TPU v7x, 512 devices: a whole 4x8x8 slice. The times are simulated.
512 devices in a mesh: space: 128 (over x, y, z_hi, core), modes: 4 (over z_lo).
Axes of the slice: x: 4, y: 8, z: 8 (z_hi: 2, z_lo: 4; z = z_hi * 4 + z_lo), core: 2. Of those that a mesh axis runs over, the one named last changes fastest.
Arguments:
- voltage_expansion: float32 [220, 128, 2048], P('modes', 'space'), may hold values from -6 to 6
- current_injection: float32 [220, 128, 2048], P('modes', 'space'), may hold values from -48 to 48
- thermal_state: float32 [220, 128, 2048], P('modes', 'space'), may hold values from -6 to 6
- average_electric_transport: float32 [128, 2048], P('space'), may hold values from 0.5 to 4
- material_zone: int32 [128, 2048], P('space'), may hold values from 0 to 3
- zone_relative_response: float32 [4, 9], replicated, may hold values from 0.02 to 0.12
- polynomial_exponent_rows: int32 [220, 9], replicated, may hold values from 0 to 3, as said below
- quadrature_abscissa_choice: int32 [512, 9], replicated, may hold values from 0 to 4
- quadrature_integer_share: int32 [512], replicated, may hold values from 1 to 1024
Outputs:
- relaxed_voltage: float32 [220, 128, 2048], P('modes', 'space')
- advanced_thermal_state: float32 [220, 128, 2048], P('modes', 'space')
Inputs may be any that keep to these rules, and one draw needn't show every extreme that they name: `polynomial_exponent_rows`: the rows are the 220 multi-indices of total degree at most 3 over 9 parameters, each once.
All inputs are finite; a program needn't handle non-finite values.
Results may differ from a plain program's by a relative error of at most 0.0003.
Values sent between devices are 32-bit elements; how exact they have to be, the bound alone decides.
A program may use at most 64 MiB of HBM per device.

v0:
```python
import jax
import jax.numpy as jnp
from jax import lax
from jax.sharding import PartitionSpec as P

NY = 256
NZ = 8
HERMITE_NODES = (
    0.0,
    1.355626179974266,
    -1.355626179974266,
    2.8569700138728056,
    -2.8569700138728056,
)


def padded_2(block, sides, width):
    for axis, dim in sides:
        count = lax.axis_size(axis)
        forward = [(i, i + 1) for i in range(count - 1)]
        backward = [(target, source) for source, target in forward]
        low = lax.ppermute(
            lax.slice_in_dim(block, block.shape[dim] - width, None, axis=dim), axis, forward
        )
        high = lax.ppermute(lax.slice_in_dim(block, 0, width, axis=dim), axis, backward)
        block = jnp.concatenate([low, block, high], axis=dim)
    return block


def neighbours(field):
    column_ids = jnp.arange(field.shape[-1])
    depth_pos = column_ids % NZ
    row_pos = column_ids // NZ
    z_next = jnp.where(depth_pos < NZ - 1, jnp.roll(field, -1, -1), 0.0)
    z_prev = jnp.where(depth_pos > 0, jnp.roll(field, 1, -1), 0.0)
    y_next = jnp.where(row_pos < NY - 1, jnp.roll(field, -NZ, -1), 0.0)
    y_prev = jnp.where(row_pos > 0, jnp.roll(field, NZ, -1), 0.0)
    return (z_next, z_prev, y_next, y_prev)


def diffusion_operator_weights(padded):
    center = padded[..., 1:-1, :]
    z_next, z_prev, y_next, y_prev = neighbours(center)
    return (
        6.0 * center - padded[..., 2:, :] - padded[..., :-2, :] - z_next - z_prev - y_next - y_prev
    )


def gradient(padded):
    center = padded[..., 1:-1, :]
    z_next, z_prev, y_next, y_prev = neighbours(center)
    along_x = (padded[..., 2:, :] - padded[..., :-2, :]) * 0.5
    along_y = (y_next - y_prev) * 0.5
    along_z = (z_next - z_prev) * 0.5
    return jnp.stack([along_x, along_y, along_z])


def coupling(row_table, col_table):
    offsets = row_table[:, None, :] - col_table[None, :, :]
    differ_count = jnp.sum((offsets != 0).astype(jnp.int32), axis=2)
    layers = [jnp.where(differ_count == 0, 1.0, 0.0).astype(jnp.float32)]
    for which_param in range(row_table.shape[1]):
        larger = jnp.maximum(
            row_table[:, None, which_param], col_table[None, :, which_param]
        ).astype(jnp.float32)
        linked = (jnp.abs(offsets[:, :, which_param]) == 1) & (differ_count == 1)
        layers.append(jnp.where(linked, jnp.sqrt(larger), 0.0))
    return jnp.stack(layers)


def node_values(quadrature_abscissa_choice):
    node_vals = jnp.zeros(quadrature_abscissa_choice.shape, jnp.float32)
    for which_node in range(5):
        node_vals = node_vals + jnp.where(
            quadrature_abscissa_choice == which_node, HERMITE_NODES[which_node], 0.0
        )
    return node_vals


def basis_values(polynomial_exponent_rows, node_vals):
    poly_terms = [
        jnp.ones_like(node_vals),
        node_vals,
        (node_vals * node_vals - 1.0) / jnp.sqrt(2.0),
        (node_vals * node_vals * node_vals - 3.0 * node_vals) / jnp.sqrt(6.0),
    ]
    basis_vals = jnp.ones((node_vals.shape[0], polynomial_exponent_rows.shape[0]), jnp.float32)
    for which_param in range(polynomial_exponent_rows.shape[1]):
        degree = polynomial_exponent_rows[:, which_param]
        factor = jnp.zeros_like(basis_vals)
        for which_deg in range(4):
            factor = factor + jnp.where(
                degree[None, :] == which_deg, poly_terms[which_deg][:, which_param][:, None], 0.0
            )
        basis_vals = basis_vals * factor
    return basis_vals


def on_device(
    voltage_expansion,
    current_injection,
    thermal_state,
    average_electric_transport,
    material_zone,
    zone_relative_response,
    polynomial_exponent_rows,
    quadrature_abscissa_choice,
    quadrature_integer_share,
):
    hp = lax.Precision.HIGHEST
    modes_here = voltage_expansion.shape[0]
    planes = voltage_expansion.shape[1]
    columns = voltage_expansion.shape[2]
    cell_count = planes * columns
    nreg = zone_relative_response.shape[0]
    all_modes = polynomial_exponent_rows.shape[0]
    num_points = quadrature_integer_share.shape[0]
    first_mode = lax.axis_index("modes") * modes_here
    own_table = lax.dynamic_slice_in_dim(polynomial_exponent_rows, first_mode, modes_here, 0)
    bordered_quantities = padded_2(
        jnp.stack([voltage_expansion, thermal_state]), (("space", 2),), 1
    )
    pot_padded = bordered_quantities[0]
    thermal_state_bordered = bordered_quantities[1]
    sens_cell = jnp.zeros((zone_relative_response.shape[1],) + material_zone.shape, jnp.float32)
    for which_region in range(nreg):
        sens_cell = sens_cell + jnp.where(
            material_zone[None] == which_region,
            zone_relative_response[which_region][:, None, None],
            0.0,
        )
    coeff = (
        jnp.concatenate([jnp.ones((1,) + material_zone.shape, jnp.float32), sens_cell])
        * average_electric_transport
    )
    coeff_flat = coeff.reshape(coeff.shape[0], cell_count)
    flat_rough = diffusion_operator_weights(pot_padded).reshape(modes_here, cell_count)
    row_coup = coupling(own_table, polynomial_exponent_rows)
    mixed = jnp.einsum(
        "mij,jc->mic",
        row_coup,
        lax.all_gather(flat_rough, "modes", axis=0, tiled=True),
        precision=hp,
    )
    applied = jnp.sum(coeff_flat[:, None, :] * mixed, axis=0)
    applied = applied.reshape(modes_here, planes, columns)
    relaxed_voltage = voltage_expansion + 0.8 * (current_injection - applied) / (
        6.0 * average_electric_transport
    )
    node_vals = node_values(quadrature_abscissa_choice)
    basis_vals = basis_values(polynomial_exponent_rows, node_vals)
    new_padded = padded_2(relaxed_voltage, (("space", 1),), 1)
    grads = gradient(new_padded)
    point_grads = jnp.einsum(
        "qi,kixn->kqxn",
        basis_vals,
        lax.all_to_all(grads, "modes", split_axis=3, concat_axis=1, tiled=True),
        precision=hp,
    )
    quarter = columns // lax.axis_size("modes")
    offset = lax.axis_index("modes") * quarter
    cond_part = lax.dynamic_slice_in_dim(average_electric_transport, offset, quarter, 1)
    region_part = lax.dynamic_slice_in_dim(material_zone, offset, quarter, 1)
    cond_lift = 1.0 + jnp.dot(zone_relative_response, node_vals.T, precision=hp)
    spread = jnp.zeros((num_points, planes, quarter), jnp.float32)
    for which_region in range(nreg):
        spread = spread + jnp.where(
            region_part[None] == which_region, cond_lift[which_region][:, None, None], 0.0
        )
    joule_heat = cond_part * spread * jnp.sum(point_grads * point_grads, axis=0)
    weighted = (
        basis_vals.T
        * quadrature_integer_share[None, :].astype(jnp.float32)
        / (512.0 * num_points * all_modes)
    )
    heat_points = jnp.einsum("iq,qxn->ixn", weighted, joule_heat, precision=hp)
    thermal_expansion_terms = lax.all_to_all(
        heat_points, "modes", split_axis=0, concat_axis=2, tiled=True
    )
    advanced_thermal_state = thermal_state + 0.1 * (
        thermal_expansion_terms - 1.5 * diffusion_operator_weights(thermal_state_bordered)
    )
    return (relaxed_voltage, advanced_thermal_state)


def solution(mesh):
    in_specs = (
        P("modes", "space", None),
        P("modes", "space", None),
        P("modes", "space", None),
        P("space", None),
        P("space", None),
        P(),
        P(),
        P(),
        P(),
    )
    out_specs = (P("modes", "space", None), P("modes", "space", None))
    return jax.shard_map(
        on_device, mesh=mesh, in_specs=in_specs, out_specs=out_specs, check_vma=False
    )
```

profile of v0, /device:TPU:59, one launch (start us, length us, event | category | flops | bytes accessed | tf_op | source)
XLA Modules:
  0.0 265.5 jit_solution(5457627602112726379)
XLA Ops:
  7.2 1.4 copy_bitcast_fusion
  8.8 0.7 copy.62
  9.5 2.6 collective-permute-start.1
  12.1 10.5 %collective-permute-start = (f32[2,55,1,2048]{3,0,2,1:T(2,128)S(1)}, f32[2,55,1,2048]{3,0,2,1:T(2,128)}, u32[]{:S(2)}, u32[]{:S(2)}) collective-permute-start(f32[2,55,1,2048]{3,0,2,1:T(2,128)S(1)} %copy.62), channel_id=1, source_target_pairs={{0,4},{4,8},{8,12},{12,16},{16,20},{20,24},{24,28},{28,32},{32,36}... | collective-permute-start | bytes 2703368 | tf_op jit(solution)/shard_map/ppermute | solution.py:22
  22.9 0.1 broadcast_subtract_fusion
  23.0 0.6 bitcast_dynamic-update-slice_fusion
  23.8 0.6 compare_reduce_fusion.7
  24.5 0.7 select_dynamic-update-slice_fusion.8
  25.2 0.7 select_dynamic-update-slice_fusion.7
  25.9 0.7 select_dynamic-update-slice_fusion.6
  26.7 0.7 select_dynamic-update-slice_fusion.5
  27.4 27.7 %collective-permute-done.1 = f32[2,55,1,2048]{3,0,2,1:T(2,128)} collective-permute-done((f32[2,55,1,2048]{3,0,2,1:T(2,128)S(1)}, f32[2,55,1,2048]{3,0,2,1:T(2,128)}, u32[]{:S(2)}, u32[]{:S(2)}) %collective-permute-start.1) | collective-permute-done | bytes 901152 | tf_op jit(solution)/shard_map/ppermute | solution.py:25
  55.0 1.7 copy.65
  56.7 8.6 %collective-permute-done = f32[2,55,1,2048]{3,0,2,1:T(2,128)} collective-permute-done((f32[2,55,1,2048]{3,0,2,1:T(2,128)S(1)}, f32[2,55,1,2048]{3,0,2,1:T(2,128)}, u32[]{:S(2)}, u32[]{:S(2)}) %collective-permute-start) | collective-permute-done | bytes 901152 | tf_op jit(solution)/shard_map/ppermute | solution.py:22
  65.4 1.7 copy.64
  67.1 0.3 pad_maximum_fusion
  67.3 0.2 slice_bitcast_fusion
  67.6 0.2 fusion.347
  67.9 0.2 fusion.345
  68.1 0.4 fusion.32
  68.5 1.2 copy.66
  69.8 0.5 broadcast_compare_fusion.27
  70.3 0.7 select_dynamic-update-slice_fusion.4
  71.1 0.7 select_dynamic-update-slice_fusion.3
  71.8 0.7 select_dynamic-update-slice_fusion.2
  72.5 0.7 select_dynamic-update-slice_fusion.1
  73.2 0.7 select_dynamic-update-slice_fusion
  73.9 0.1 select_add_fusion
  74.1 42.7 %all-gather.3.cloned.1.call-done = f32[220,1,2048]{2,1,0:T(1,128)} async-done(((f32[55,1,2048]{2,1,0:T(1,128)}), f32[220,1,2048]{2,1,0:T(1,128)}) %all-gather.3.cloned.1.call-update) | async-done | bytes 1802256 | tf_op jit(solution)/shard_map/all_gather | solution.py:142
  116.8 5.9 %multiply_reduce_fusion = f32[55,2048]{1,0:T(8,128)S(1)} fusion(f32[10,55,220]{2,1,0:T(8,128)} %select_dynamic-update-slice_fusion, f32[10,2048]{1,0:T(8,128)S(1)} %multiply_bitcast_fusion.1, f32[220,1,2048]{2,1,0:T(1,128)} %all-gather.3.cloned.1.call-done), kind=kOutput, calls=%fused_computation | convolution fusion | flops 2975836160 | bytes 2818720 | tf_op jit(solution)/shard_map/mij,jc->mic/dot_general | solution.py:139
  122.8 0.4 fusion.40
  123.2 0.2 slice_bitcast_fusion.2
  123.5 0.2 slice_bitcast_fusion.4
  123.7 3.1 %collective-permute-start.2 = (f32[55,1,2048]{2,0,1:T(8,128)S(1)}, f32[55,1,2048]{2,0,1:T(8,128)S(1)}, u32[]{:S(2)}, u32[]{:S(2)}) collective-permute-start(f32[55,1,2048]{2,0,1:T(8,128)S(1)} %fusion.40), channel_id=1, source_target_pairs={{4,0},{8,4},{12,8},{16,12},{20,16},{24,20},{28,24},{32,28},{36,32}... | collective-permute-start | bytes 1351688 | tf_op jit(solution)/shard_map/ppermute | solution.py:25
  126.8 6.6 %collective-permute-start.3 = (f32[55,1,2048]{2,0,1:T(8,128)S(1)}, f32[55,1,2048]{2,0,1:T(8,128)S(1)}, u32[]{:S(2)}, u32[]{:S(2)}) collective-permute-start(f32[55,1,2048]{2,0,1:T(8,128)S(1)} %fusion.40), channel_id=1, source_target_pairs={{0,4},{4,8},{8,12},{12,16},{16,20},{20,24},{24,28},{28,32},{32,36}... | collective-permute-start | bytes 1351688 | tf_op jit(solution)/shard_map/ppermute | solution.py:22
  133.3 0.2 fusion.36
  133.5 0.2 fusion.34
  133.7 9.7 %collective-permute-done.2 = f32[55,1,2048]{2,0,1:T(8,128)S(1)} collective-permute-done((f32[55,1,2048]{2,0,1:T(8,128)S(1)}, f32[55,1,2048]{2,0,1:T(8,128)S(1)}, u32[]{:S(2)}, u32[]{:S(2)}) %collective-permute-start.2) | collective-permute-done | bytes 450592 | tf_op jit(solution)/shard_map/ppermute | solution.py:25
  143.4 11.2 %collective-permute-done.3 = f32[55,1,2048]{2,0,1:T(8,128)S(1)} collective-permute-done((f32[55,1,2048]{2,0,1:T(8,128)S(1)}, f32[55,1,2048]{2,0,1:T(8,128)S(1)}, u32[]{:S(2)}, u32[]{:S(2)}) %collective-permute-start.3) | collective-permute-done | bytes 450592 | tf_op jit(solution)/shard_map/ppermute | solution.py:22
  154.8 3.1 %copy.71 = f32[3,55,1,2048]{1,0,2,3:T(4,128)} copy(f32[3,55,1,2048]{3,1,2,0:T(8,128)S(1)} %pad_maximum_fusion.1) | data formatting | bytes 2703360 | tf_op jit(solution)/shard_map/stack | solution.py:55
  157.9 6.6 %reshape.2106 = f32[4,1,84480]{2,1,0:T(1,128)} reshape(f32[2048,1,3,55]{3,2,1,0:T(4,128)} %bitcast.196) | data formatting | bytes 2703360
  164.6 3.7 %all-to-all-start = ((f32[4,1,84480]{2,1,0:T(1,128)}), f32[4,1,84480]{2,1,0:T(1,128)S(1)}, u32[]{:S(2)}, u32[]{:S(2)}) async-start(f32[4,1,84480]{2,1,0:T(1,128)} %reshape.2106), calls=%async_computation | async-start | bytes 2703360 | tf_op jit(solution)/shard_map/all_to_all | solution.py:157
  168.3 0.2 fusion.2
  168.6 1.1 fusion.343
  169.7 29.8 %all-to-all-done = f32[4,1,84480]{2,1,0:T(1,128)S(1)} async-done(((f32[4,1,84480]{2,1,0:T(1,128)}), f32[4,1,84480]{2,1,0:T(1,128)S(1)}, u32[]{:S(2)}, u32[]{:S(2)}) %all-to-all-start) | async-done | bytes 1351712 | tf_op jit(solution)/shard_map/all_to_all | solution.py:157
  199.6 0.5 broadcast.1558
  200.1 5.6 %reduce.20 = f32[4,84480]{1,0:T(4,128)} reduce(f32[4,1,84480]{2,1,0:T(1,128)S(1)} %all-to-all-done, f32[]{:T(128)} %broadcast.1558), dimensions={1}, to_apply=%all_to_all.24.reduce_sub_computation | reduce | bytes 2703364 | tf_op jit(solution)/shard_map/all_to_all | solution.py:157
  205.7 6.9 %reshape.2107 = f32[2048,1,3,55]{3,2,1,0:T(4,128)} reshape(f32[4,84480]{1,0:T(4,128)} %reduce.20) | data formatting | bytes 2703360
  212.6 4.6 %copy.79 = f32[3,55,1,4,512]{4,3,1,0,2:T(4,128)} copy(f32[3,55,1,4,512]{1,0,4,3,2:T(4,128)} %bitcast.197) | data formatting | bytes 2703360 | tf_op jit(solution)/shard_map/all_to_all | solution.py:157
  217.2 1.8 copy.73
  219.0 1.3 reshape.2092
  220.3 6.3 %multiply_reduce_fusion.1 = f32[512,512]{1,0:T(8,128)S(1)} fusion(f32[3,220,512]{2,1,0:T(8,128)} %reshape.2092, f32[512]{0:T(512)S(1)} %bitcast.231, f32[512]{0:T(512)S(1)} %bitcast.279, f32[512]{0:T(512)S(1)} %bitcast.259, f32[220]{0:T(256)S(1)} %get-tuple-element.133, f32[512]{0:T(512)S(1)} %bitcast.233, f32[512]{0:T(512)S(1)} %bitcast.277, ...), kind=kOutput, calls=%fused_computation.1 | convolution fusion | flops 2084474880 | bytes 2469412 | tf_op jit(solution)/shard_map/qi,kixn->kqxn/dot_general | solution.py:154
  226.6 3.1 %convolution_bitcast_fusion = f32[220,1,512]{2,0,1:T(8,128)S(1)} fusion(f32[512,512]{1,0:T(8,128)S(1)} %multiply_reduce_fusion.1, f32[512]{0:T(512)S(1)} %bitcast.285, f32[512]{0:T(512)S(1)} %bitcast.286, f32[512]{0:T(512)S(1)} %bitcast.287, f32[512]{0:T(512)S(1)} %bitcast.284, f32[512]{0:T(512)S(1)} %bitcast.283, pred[512]{0:T(512)(128)(4,1)S(1)} %copy-done.13, ...), kind=kOutput, calls=%fused_computation.8 | convolution fusion | flops 701628416 | bytes 1582628 | tf_op jit(solution)/shard_map/iq,qxn->ixn/dot_general | solution.py:176
  229.7 1.2 copy.74
  230.9 3.7 %all-to-all-start.1 = ((f32[220,1,512]{2,1,0:T(1,128)}), f32[220,1,512]{2,1,0:T(1,128)S(1)}, u32[]{:S(2)}, u32[]{:S(2)}) async-start(f32[220,1,512]{2,1,0:T(1,128)} %copy.74), calls=%async_computation.1 | async-start | bytes 901120 | tf_op jit(solution)/shard_map/all_to_all | solution.py:177
  234.7 0.2 fusion.341
  234.9 1.2 copy.77
  236.2 11.5 %all-to-all-done.1 = f32[220,1,512]{2,1,0:T(1,128)S(1)} async-done(((f32[220,1,512]{2,1,0:T(1,128)}), f32[220,1,512]{2,1,0:T(1,128)S(1)}, u32[]{:S(2)}, u32[]{:S(2)}) %all-to-all-start.1) | async-done | bytes 450592 | tf_op jit(solution)/shard_map/all_to_all | solution.py:177
  247.7 1.9 reduce.11
  249.6 1.9 all_to_all.28
  251.6 2.1 copy.75
  253.6 2.1 all_to_all.30
  255.7 1.7 fusion.28
  257.4 1.2 copy.78
  (69 shorter events, 1.3 us)
Async XLA Ops:
  7.2 109.7 %all-gather.3.cloned.1.call-start = ((), (), s32[]{:S(2)}) async-start(), calls=%async_computation.2 | async-start | bytes 2252800 | tf_op jit(solution)/shard_map/all_gather | solution.py:142
  8.7 14.0 %copy-start.4 = (s32[220,9]{0,1:T(8,128)S(1)}, s32[220,9]{0,1:T(8,128)}, u32[]{:S(2)}) copy-start(s32[220,9]{0,1:T(8,128)} %param.15) | copy-start | bytes 23764
  8.7 14.9 %copy-start.7 = (s32[1,2048]{1,0:T(1,128)S(1)}, s32[1,2048]{1,0:T(1,128)}, u32[]{:S(2)}) copy-start(s32[1,2048]{1,0:T(1,128)} %param.13) | copy-start | bytes 24580
  8.8 15.6 %copy-start.5 = (f32[1,2048]{1,0:T(1,128)S(1)}, f32[1,2048]{1,0:T(1,128)}, u32[]{:S(2)}) copy-start(f32[1,2048]{1,0:T(1,128)} %param.12) | copy-start | bytes 24580
  8.8 15.6 %copy-start.8 = (s32[512]{0:T(512)S(1)}, s32[512]{0:T(512)}, u32[]{:S(2)}) copy-start(s32[512]{0:T(512)} %param.17) | copy-start | bytes 6148
  8.8 16.4 %copy-start.9 = (f32[4,9]{1,0:T(4,128)S(1)}, f32[4,9]{1,0:T(4,128)}, u32[]{:S(2)}) copy-start(f32[4,9]{1,0:T(4,128)} %param.14) | copy-start | bytes 436
  9.5 45.6 %collective-permute-start.1 = (f32[2,55,1,2048]{3,0,2,1:T(2,128)S(1)}, f32[2,55,1,2048]{3,0,2,1:T(2,128)}, u32[]{:S(2)}, u32[]{:S(2)}) collective-permute-start(f32[2,55,1,2048]{3,0,2,1:T(2,128)S(1)} %copy.62), channel_id=1, source_target_pairs={{4,0},{8,4},{12,8},{16,12},{20,16},{24,20},{28,24},{32,28},{36,32}... | collective-permute-start | bytes 2703368 | tf_op jit(solution)/shard_map/ppermute | solution.py:25
  12.1 53.3 %collective-permute-start = (f32[2,55,1,2048]{3,0,2,1:T(2,128)S(1)}, f32[2,55,1,2048]{3,0,2,1:T(2,128)}, u32[]{:S(2)}, u32[]{:S(2)}) collective-permute-start(f32[2,55,1,2048]{3,0,2,1:T(2,128)S(1)} %copy.62), channel_id=1, source_target_pairs={{0,4},{4,8},{8,12},{12,16},{16,20},{20,24},{24,28},{28,32},{32,36}... | collective-permute-start | bytes 2703368 | tf_op jit(solution)/shard_map/ppermute | solution.py:22
  74.1 48.7 %copy-start.2 = (f32[55,1,2048]{2,1,0:T(1,128)S(1)}, f32[55,1,2048]{2,1,0:T(1,128)}, u32[]{:S(2)}) copy-start(f32[55,1,2048]{2,1,0:T(1,128)} %param.9) | copy-start | bytes 1351684
  74.1 48.7 %copy-start.3 = (f32[55,1,2048]{2,1,0:T(1,128)S(1)}, f32[55,1,2048]{2,1,0:T(1,128)}, u32[]{:S(2)}) copy-start(f32[55,1,2048]{2,1,0:T(1,128)} %param.10) | copy-start | bytes 1351684
  123.7 19.7 %collective-permute-start.2 = (f32[55,1,2048]{2,0,1:T(8,128)S(1)}, f32[55,1,2048]{2,0,1:T(8,128)S(1)}, u32[]{:S(2)}, u32[]{:S(2)}) collective-permute-start(f32[55,1,2048]{2,0,1:T(8,128)S(1)} %fusion.40), channel_id=1, source_target_pairs={{4,0},{8,4},{12,8},{16,12},{20,16},{24,20},{28,24},{32,28},{36,32}... | collective-permute-start | bytes 1351688 | tf_op jit(solution)/shard_map/ppermute | solution.py:25
  126.8 27.9 %collective-permute-start.3 = (f32[55,1,2048]{2,0,1:T(8,128)S(1)}, f32[55,1,2048]{2,0,1:T(8,128)S(1)}, u32[]{:S(2)}, u32[]{:S(2)}) collective-permute-start(f32[55,1,2048]{2,0,1:T(8,128)S(1)} %fusion.40), channel_id=1, source_target_pairs={{0,4},{4,8},{8,12},{12,16},{16,20},{20,24},{24,28},{28,32},{32,36}... | collective-permute-start | bytes 1351688 | tf_op jit(solution)/shard_map/ppermute | solution.py:22
  164.6 3.7 %copy-start.6 = (s32[512,9]{0,1:T(8,128)S(1)}, s32[512,9]{0,1:T(8,128)}, u32[]{:S(2)}) copy-start(s32[512,9]{0,1:T(8,128)} %param.16) | copy-start | bytes 55300
  164.6 35.0 %all-to-all-start = ((f32[4,1,84480]{2,1,0:T(1,128)}), f32[4,1,84480]{2,1,0:T(1,128)S(1)}, u32[]{:S(2)}, u32[]{:S(2)}) async-start(f32[4,1,84480]{2,1,0:T(1,128)} %reshape.2106), calls=%async_computation | async-start | bytes 2703360 | tf_op jit(solution)/shard_map/all_to_all | solution.py:157
  220.2 6.3 %copy-start.10 = (pred[512]{0:T(512)(128)(4,1)S(1)}, pred[512]{0:T(512)(128)(4,1)}, u32[]{:S(2)}) copy-start(pred[512]{0:T(512)(128)(4,1)} %get-tuple-element.12) | copy-start | bytes 1540
  220.2 6.3 %copy-start.11 = (pred[512]{0:T(512)(128)(4,1)S(1)}, pred[512]{0:T(512)(128)(4,1)}, u32[]{:S(2)}) copy-start(pred[512]{0:T(512)(128)(4,1)} %get-tuple-element.13) | copy-start | bytes 1540
  220.3 6.3 %copy-start.12 = (pred[512]{0:T(512)(128)(4,1)S(1)}, pred[512]{0:T(512)(128)(4,1)}, u32[]{:S(2)}) copy-start(pred[512]{0:T(512)(128)(4,1)} %get-tuple-element.14) | copy-start | bytes 1540
  220.3 6.3 %copy-start.13 = (pred[512]{0:T(512)(128)(4,1)S(1)}, pred[512]{0:T(512)(128)(4,1)}, u32[]{:S(2)}) copy-start(pred[512]{0:T(512)(128)(4,1)} %get-tuple-element.15) | copy-start | bytes 1540
  220.3 6.3 %copy-start.14 = (pred[220]{0:T(512)(128)(4,1)S(1)}, pred[220]{0:T(512)(128)(4,1)}, u32[]{:S(2)}) copy-start(pred[220]{0:T(512)(128)(4,1)} %get-tuple-element.106) | copy-start | bytes 664
  220.3 6.3 %copy-start.15 = (pred[220]{0:T(512)(128)(4,1)S(1)}, pred[220]{0:T(512)(128)(4,1)}, u32[]{:S(2)}) copy-start(pred[220]{0:T(512)(128)(4,1)} %get-tuple-element.107) | copy-start | bytes 664
  220.3 6.3 %copy-start.16 = (pred[220]{0:T(512)(128)(4,1)S(1)}, pred[220]{0:T(512)(128)(4,1)}, u32[]{:S(2)}) copy-start(pred[220]{0:T(512)(128)(4,1)} %get-tuple-element.108) | copy-start | bytes 664
  230.9 16.8 %all-to-all-start.1 = ((f32[220,1,512]{2,1,0:T(1,128)}), f32[220,1,512]{2,1,0:T(1,128)S(1)}, u32[]{:S(2)}, u32[]{:S(2)}) async-start(f32[220,1,512]{2,1,0:T(1,128)} %copy.74), calls=%async_computation.1 | async-start | bytes 901120 | tf_op jit(solution)/shard_map/all_to_all | solution.py:177
  249.6 6.1 %copy-start = (f32[55,1,2047]{2,0,1:T(8,128)S(1)}, f32[55,1,2047]{2,0,1:T(8,128)}, u32[]{:S(2)}) copy-start(f32[55,1,2047]{2,0,1:T(8,128)} %get-tuple-element.30) | copy-start | bytes 1351024
  249.6 6.1 %copy-start.1 = (f32[55,1,2047]{2,0,1:T(8,128)S(1)}, f32[55,1,2047]{2,0,1:T(8,128)}, u32[]{:S(2)}) copy-start(f32[55,1,2047]{2,0,1:T(8,128)} %get-tuple-element.31) | copy-start | bytes 1351024
Sparse Core Ops, SparseCore 0:
  69.9 46.8 all-gather.2
where the time goes:
time: 266 us
  waiting for transfers between devices  141 us (53%)
  local copies, waits for them, and re-layouts  44.4 us (17%)
  starting transfers between devices  30.2 us (11%)
  other arithmetic  19.7 us (7%)
  matrix products  15.4 us (6%)
  between operations  14.5 us (5%)
    all_gather x1, waiting for transfers between devices, on_device(): lax.all_gather(flat_rough, 'modes', axis=0, tiled=True)  42.7 us
    ppermute x2, waiting for transfers between devices, padded_2(): lax.ppermute(lax.slice_in_dim(block, 0, width, axis=dim), axis, backward)  37.3 us
    all_to_all x1, waiting for transfers between devices, on_device(): lax.all_to_all(grads, 'modes', split_axis=3, concat_axis=1, tiled=True)  29.8 us
    ppermute x2, waiting for transfers between devices, padded_2(): lax.ppermute(lax.slice_in_dim(block, block.shape[dim] - width, None, axis...  19.9 us
    unnamed x39, local copies, waits for them, and re-layouts  17.5 us
    ppermute x2, starting transfers between devices, padded_2(): lax.ppermute(lax.slice_in_dim(block, block.shape[dim] - width, None, axis...  17.1 us
    all_to_all x1, waiting for transfers between devices, on_device(): lax.all_to_all(heat_points, 'modes', split_axis=0, concat_axis=2, tiled=T...  11.5 us
    all_to_all x3, local copies, waits for them, and re-layouts, on_device(): lax.all_to_all(grads, 'modes', split_axis=3, concat_axis=1, tiled=True)  6.9 us
  transfers between devices with their start and end apart: 7, of which 7 were waited for; matrix products, arithmetic and copies ran while one was open for 5% of the time, Pallas kernels for 0%

commit v1 on v0

--- a/solution.py
+++ b/solution.py
@@ -154,7 +154,12 @@
     point_grads = jnp.einsum(
         "qi,kixn->kqxn",
         basis_vals,
-        lax.all_to_all(grads, "modes", split_axis=3, concat_axis=1, tiled=True),
+        jnp.concatenate(
+            lax.all_to_all(
+                jnp.stack(jnp.split(grads, lax.axis_size("modes"), axis=3)), "modes", 0, 0
+            ),
+            axis=1,
+        ),
         precision=hp,
     )
     quarter = columns // lax.axis_size("modes")

time: 266 us -> 246 us (0.925)
  local copies, waits for them, and re-layouts: 44.4 us -> 24.7 us
    ppermute x2, waiting for transfers between devices: 37.3 us -> 5.25 us  [padded_2(): lax.ppermute(lax.slice_in_dim(block, 0, width, axis=dim), axis, backward)]
    ppermute x2, waiting for transfers between devices: 19.9 us -> 45.1 us  [padded_2(): lax.ppermute(lax.slice_in_dim(block, block.shape[dim] - width, None, axis...]
    unnamed x39 -> x38, local copies, waits for them, and re-layouts: 17.5 us -> 3.85 us
    all_to_all x3 -> x0, local copies, waits for them, and re-layouts: 6.9 us -> none  [on_device(): lax.all_to_all(grads, 'modes', split_axis=3, concat_axis=1, tiled=True)]
    all_to_all x1 -> x0, other arithmetic: 5.65 us -> none  [on_device(): lax.all_to_all(grads, 'modes', split_axis=3, concat_axis=1, tiled=True)]
    all_gather x1, waiting for transfers between devices: 42.7 us -> 46 us  [on_device(): lax.all_gather(flat_rough, 'modes', axis=0, tiled=True)]
  transfers between devices with their start and end apart: 7 -> 7, of which waited for: 7 -> 6; matrix products, arithmetic and copies ran while one was open for 5% -> 7% of each run, Pallas kernels for 0% -> 0%
where the time goes in v1:
time: 246 us; the launch traced here: 245 us
  waiting for transfers between devices  139 us (57%)
  starting transfers between devices  30.4 us (12%)
  local copies, waits for them, and re-layouts  24.7 us (10%)
  other arithmetic  21 us (9%)
  matrix products  15.4 us (6%)
  between operations  14.6 us (6%)
    all_gather x1, waiting for transfers between devices, on_device(): lax.all_gather(flat_rough, 'modes', axis=0, tiled=True)  46 us
    ppermute x2, waiting for transfers between devices, padded_2(): lax.ppermute(lax.slice_in_dim(block, block.shape[dim] - width, None, axis...  45.1 us
    all_to_all x1, waiting for transfers between devices, on_device(): lax.all_to_all(jnp.stack(jnp.split(grads, lax.axis_size('modes'), axis=3)...  29.9 us
    ppermute x2, starting transfers between devices, padded_2(): lax.ppermute(lax.slice_in_dim(block, block.shape[dim] - width, None, axis...  17.8 us
    all_to_all x1, waiting for transfers between devices, on_device(): lax.all_to_all(heat_points, 'modes', split_axis=0, concat_axis=2, tiled=T...  12.8 us
    unnamed x9, other arithmetic  6.35 us
    dot_general x1, matrix products, on_device(): jnp.einsum('qi,kixn->kqxn', basis_vals, jnp.concatenate(lax.all_to_all(jn...  6.25 us
    all_to_all x3, local copies, waits for them, and re-layouts, on_device(): lax.all_to_all(heat_points, 'modes', split_axis=0, concat_axis=2, tiled=T...  6.07 us
  transfers between devices with their start and end apart: 7, of which 6 were waited for; matrix products, arithmetic and copies ran while one was open for 7% of the time, Pallas kernels for 0%

profile of v1, /device:TPU:59, one launch (start us, length us, event | category | flops | bytes accessed | tf_op | source)
XLA Modules:
  0.0 245.1 jit_solution(8144154023790402048)
XLA Ops:
  7.2 1.4 copy_bitcast_fusion
  8.8 0.7 copy.34
  9.5 11.2 %collective-permute-start = (f32[2,55,1,2048]{3,0,2,1:T(2,128)S(1)}, f32[2,55,1,2048]{3,0,2,1:T(2,128)}, u32[]{:S(2)}, u32[]{:S(2)}) collective-permute-start(f32[2,55,1,2048]{3,0,2,1:T(2,128)S(1)} %copy.34), channel_id=1, source_target_pairs={{0,4},{4,8},{8,12},{12,16},{16,20},{20,24},{24,28},{28,32},{32,36}... | collective-permute-start | bytes 2703368 | tf_op jit(solution)/shard_map/ppermute | solution.py:22
  20.7 1.9 collective-permute-start.1
  22.9 0.1 broadcast_subtract_fusion
  23.0 0.6 bitcast_dynamic-update-slice_fusion
  23.8 0.6 compare_reduce_fusion.7
  24.4 0.1 dynamic-slice_bitcast_fusion
  24.5 0.7 select_dynamic-update-slice_fusion.8
  25.2 0.7 select_dynamic-update-slice_fusion.7
  25.9 0.7 select_dynamic-update-slice_fusion.6
  26.7 0.7 select_dynamic-update-slice_fusion.5
  27.4 33.9 %collective-permute-done = f32[2,55,1,2048]{3,0,2,1:T(2,128)} collective-permute-done((f32[2,55,1,2048]{3,0,2,1:T(2,128)S(1)}, f32[2,55,1,2048]{3,0,2,1:T(2,128)}, u32[]{:S(2)}, u32[]{:S(2)}) %collective-permute-start) | collective-permute-done | bytes 901152 | tf_op jit(solution)/shard_map/ppermute | solution.py:22
  61.3 1.7 copy.36
  63.0 1.7 copy.37
  64.7 0.3 pad_maximum_fusion
  65.0 0.2 slice_bitcast_fusion
  65.2 0.2 fusion.342
  65.4 0.2 fusion.344
  65.7 0.5 fusion.32
  66.2 1.2 copy.38
  67.4 0.5 broadcast_compare_fusion.27
  68.0 0.7 select_dynamic-update-slice_fusion.4
  68.7 0.7 select_dynamic-update-slice_fusion.3
  69.4 0.7 select_dynamic-update-slice_fusion.2
  70.1 0.7 select_dynamic-update-slice_fusion.1
  70.8 0.7 select_dynamic-update-slice_fusion
  71.6 0.1 select_add_fusion
  71.7 46.0 %all-gather.3.cloned.1.call-done = f32[220,1,2048]{2,1,0:T(1,128)} async-done(((f32[55,1,2048]{2,1,0:T(1,128)}), f32[220,1,2048]{2,1,0:T(1,128)}) %all-gather.3.cloned.1.call-update) | async-done | bytes 1802256 | tf_op jit(solution)/shard_map/all_gather | solution.py:142
  117.8 5.9 %multiply_reduce_fusion = f32[55,2048]{1,0:T(8,128)S(1)} fusion(f32[10,55,220]{2,1,0:T(8,128)} %select_dynamic-update-slice_fusion, f32[10,2048]{1,0:T(8,128)S(1)} %multiply_bitcast_fusion.1, f32[220,1,2048]{2,1,0:T(1,128)} %all-gather.3.cloned.1.call-done), kind=kOutput, calls=%fused_computation | convolution fusion | flops 2975836160 | bytes 2818720 | tf_op jit(solution)/shard_map/mij,jc->mic/dot_general | solution.py:139
  123.7 0.9 divide_add_fusion
  124.6 3.1 %collective-permute-start.2 = (f32[55,1,2048]{2,1,0:T(1,128)S(1)}, f32[55,1,2048]{2,1,0:T(1,128)S(1)}, u32[]{:S(2)}, u32[]{:S(2)}) collective-permute-start(f32[55,1,2048]{2,1,0:T(1,128)S(1)} %divide_add_fusion), channel_id=1, source_target_pairs={{4,0},{8,4},{12,8},{16,12},{20,16},{24,20},{28,24},{32,28},{36,32}... | collective-permute-start | bytes 1351688 | tf_op jit(solution)/shard_map/ppermute | solution.py:25
  127.7 6.6 %collective-permute-start.3 = (f32[55,1,2048]{2,1,0:T(1,128)S(1)}, f32[55,1,2048]{2,1,0:T(1,128)S(1)}, u32[]{:S(2)}, u32[]{:S(2)}) collective-permute-start(f32[55,1,2048]{2,1,0:T(1,128)S(1)} %divide_add_fusion), channel_id=1, source_target_pairs={{0,4},{4,8},{8,12},{12,16},{16,20},{20,24},{24,28},{28,32},{32,36}... | collective-permute-start | bytes 1351688 | tf_op jit(solution)/shard_map/ppermute | solution.py:22
  134.3 1.0 slice_bitcast_fusion.4
  135.3 0.1 slice_bitcast_fusion.12
  135.4 1.0 slice_bitcast_fusion.2
  136.4 0.1 slice_bitcast_fusion.10
  136.5 1.1 fusion.161
  137.6 1.1 fusion.163
  138.8 5.2 %collective-permute-done.2 = f32[55,1,2048]{2,1,0:T(1,128)S(1)} collective-permute-done((f32[55,1,2048]{2,1,0:T(1,128)S(1)}, f32[55,1,2048]{2,1,0:T(1,128)S(1)}, u32[]{:S(2)}, u32[]{:S(2)}) %collective-permute-start.2) | collective-permute-done | bytes 450592 | tf_op jit(solution)/shard_map/ppermute | solution.py:25
  144.0 11.2 %collective-permute-done.3 = f32[55,1,2048]{2,1,0:T(1,128)S(1)} collective-permute-done((f32[55,1,2048]{2,1,0:T(1,128)S(1)}, f32[55,1,2048]{2,1,0:T(1,128)S(1)}, u32[]{:S(2)}, u32[]{:S(2)}) %collective-permute-start.3) | collective-permute-done | bytes 450592 | tf_op jit(solution)/shard_map/ppermute | solution.py:22
  155.2 0.9 multiply_bitcast_fusion
  156.1 1.3 pad_maximum_fusion.1
  157.5 0.9 slice_bitcast_fusion.9
  158.4 2.5 %pad_maximum_fusion.2 = f32[4,3,55,1,512]{4,3,2,1,0:T(1,128)} fusion(f32[1,3,55,1,512]{4,3,2,1,0:T(1,128)S(1)} %get-tuple-element.39, f32[1,3,55,1,512]{4,3,2,1,0:T(1,128)S(1)} %get-tuple-element.40, f32[1,3,55,1,512]{4,3,2,1,0:T(1,128)S(1)} %get-tuple-element.41, f32[1,3,55,1,512]{4,3,2,1,0:T(1,128)S(1)} %get-tuple-element.38), kind=kLoop, calls=%fused_computation.8 | loop fusion | flops 1013760 | bytes 2703360 | tf_op jit(solution)/shard_map/stack | solution.py:159
  160.9 3.9 %all-to-all-start = ((f32[4,3,55,1,512]{4,3,2,1,0:T(1,128)}), f32[4,3,55,1,512]{4,3,2,1,0:T(1,128)S(1)}, u32[]{:S(2)}, u32[]{:S(2)}) async-start(f32[4,3,55,1,512]{4,3,2,1,0:T(1,128)} %pad_maximum_fusion.2), calls=%async_computation | async-start | bytes 2703360 | tf_op jit(solution)/shard_map/all_to_all | solution.py:158
  164.8 0.2 fusion.2
  165.2 1.0 fusion.338
  166.2 29.9 %all-to-all-done = f32[4,3,55,1,512]{4,3,2,1,0:T(1,128)S(1)} async-done(((f32[4,3,55,1,512]{4,3,2,1,0:T(1,128)}), f32[4,3,55,1,512]{4,3,2,1,0:T(1,128)S(1)}, u32[]{:S(2)}, u32[]{:S(2)}) %all-to-all-start) | async-done | bytes 1351712 | tf_op jit(solution)/shard_map/all_to_all | solution.py:158
  196.1 1.1 copy-done.1
  197.2 1.5 copy.41
  198.6 1.3 reshape.2097
  199.9 6.3 %multiply_reduce_fusion.1 = f32[512,512]{1,0:T(8,128)S(1)} fusion(f32[3,220,512]{2,1,0:T(8,128)} %reshape.2097, f32[512]{0:T(512)S(1)} %bitcast.226, f32[512]{0:T(512)S(1)} %bitcast.274, f32[512]{0:T(512)S(1)} %bitcast.254, f32[220]{0:T(256)S(1)} %get-tuple-element.135, f32[512]{0:T(512)S(1)} %bitcast.228, f32[512]{0:T(512)S(1)} %bitcast.272, ...), kind=kOutput, calls=%fused_computation.1 | convolution fusion | flops 2084474880 | bytes 2469412 | tf_op jit(solution)/shard_map/qi,kixn->kqxn/dot_general | solution.py:154
  206.3 3.1 %convolution_bitcast_fusion = f32[220,1,512]{2,0,1:T(8,128)S(1)} fusion(f32[512,512]{1,0:T(8,128)S(1)} %multiply_reduce_fusion.1, f32[512]{0:T(512)S(1)} %bitcast.280, f32[512]{0:T(512)S(1)} %bitcast.281, f32[512]{0:T(512)S(1)} %bitcast.282, f32[512]{0:T(512)S(1)} %bitcast.279, f32[512]{0:T(512)S(1)} %bitcast.278, pred[512]{0:T(512)(128)(4,1)S(1)} %copy-done.14, ...), kind=kOutput, calls=%fused_computation.9 | convolution fusion | flops 701628416 | bytes 1582628 | tf_op jit(solution)/shard_map/iq,qxn->ixn/dot_general | solution.py:181
  209.4 1.2 copy.42
  210.6 3.7 %all-to-all-start.1 = ((f32[220,1,512]{2,1,0:T(1,128)}), f32[220,1,512]{2,1,0:T(1,128)S(1)}, u32[]{:S(2)}, u32[]{:S(2)}) async-start(f32[220,1,512]{2,1,0:T(1,128)} %copy.42), calls=%async_computation.1 | async-start | bytes 901120 | tf_op jit(solution)/shard_map/all_to_all | solution.py:182
  214.4 0.2 fusion.340
  214.6 12.8 %all-to-all-done.1 = f32[220,1,512]{2,1,0:T(1,128)S(1)} async-done(((f32[220,1,512]{2,1,0:T(1,128)}), f32[220,1,512]{2,1,0:T(1,128)S(1)}, u32[]{:S(2)}, u32[]{:S(2)}) %all-to-all-start.1) | async-done | bytes 450592 | tf_op jit(solution)/shard_map/all_to_all | solution.py:182
  227.3 1.9 reduce.11
  229.3 1.9 all_to_all.18
  231.2 2.1 copy.43
  233.2 2.1 all_to_all.20
  235.3 1.7 fusion.28
  237.0 1.2 copy.45
  (66 shorter events, 0.9 us)
Async XLA Ops:
  7.2 110.6 %all-gather.3.cloned.1.call-start = ((), (), s32[]{:S(2)}) async-start(), calls=%async_computation.2 | async-start | bytes 2252800 | tf_op jit(solution)/shard_map/all_gather | solution.py:142
  8.7 14.0 %copy-start.5 = (s32[220,9]{0,1:T(8,128)S(1)}, s32[220,9]{0,1:T(8,128)}, u32[]{:S(2)}) copy-start(s32[220,9]{0,1:T(8,128)} %param.15) | copy-start | bytes 23764
  8.7 14.9 %copy-start.8 = (s32[1,2048]{1,0:T(1,128)S(1)}, s32[1,2048]{1,0:T(1,128)}, u32[]{:S(2)}) copy-start(s32[1,2048]{1,0:T(1,128)} %param.13) | copy-start | bytes 24580
  8.8 15.6 %copy-start.6 = (f32[1,2048]{1,0:T(1,128)S(1)}, f32[1,2048]{1,0:T(1,128)}, u32[]{:S(2)}) copy-start(f32[1,2048]{1,0:T(1,128)} %param.12) | copy-start | bytes 24580
  8.8 15.6 %copy-start.9 = (s32[512]{0:T(512)S(1)}, s32[512]{0:T(512)}, u32[]{:S(2)}) copy-start(s32[512]{0:T(512)} %param.17) | copy-start | bytes 6148
  8.8 16.4 %copy-start.10 = (f32[4,9]{1,0:T(4,128)S(1)}, f32[4,9]{1,0:T(4,128)}, u32[]{:S(2)}) copy-start(f32[4,9]{1,0:T(4,128)} %param.14) | copy-start | bytes 436
  9.5 51.8 %collective-permute-start = (f32[2,55,1,2048]{3,0,2,1:T(2,128)S(1)}, f32[2,55,1,2048]{3,0,2,1:T(2,128)}, u32[]{:S(2)}, u32[]{:S(2)}) collective-permute-start(f32[2,55,1,2048]{3,0,2,1:T(2,128)S(1)} %copy.34), channel_id=1, source_target_pairs={{0,4},{4,8},{8,12},{12,16},{16,20},{20,24},{24,28},{28,32},{32,36}... | collective-permute-start | bytes 2703368 | tf_op jit(solution)/shard_map/ppermute | solution.py:22
  20.7 42.3 %collective-permute-start.1 = (f32[2,55,1,2048]{3,0,2,1:T(2,128)S(1)}, f32[2,55,1,2048]{3,0,2,1:T(2,128)}, u32[]{:S(2)}, u32[]{:S(2)}) collective-permute-start(f32[2,55,1,2048]{3,0,2,1:T(2,128)S(1)} %copy.34), channel_id=1, source_target_pairs={{4,0},{8,4},{12,8},{16,12},{20,16},{24,20},{28,24},{32,28},{36,32}... | collective-permute-start | bytes 2703368 | tf_op jit(solution)/shard_map/ppermute | solution.py:25
  71.7 52.0 %copy-start.3 = (f32[55,1,2048]{2,1,0:T(1,128)S(1)}, f32[55,1,2048]{2,1,0:T(1,128)}, u32[]{:S(2)}) copy-start(f32[55,1,2048]{2,1,0:T(1,128)} %param.9) | copy-start | bytes 1351684
  71.7 52.0 %copy-start.4 = (f32[55,1,2048]{2,1,0:T(1,128)S(1)}, f32[55,1,2048]{2,1,0:T(1,128)}, u32[]{:S(2)}) copy-start(f32[55,1,2048]{2,1,0:T(1,128)} %param.10) | copy-start | bytes 1351684
  124.6 11.8 %copy-start = (f32[55,1,2048]{2,1,0:T(1,128)}, f32[55,1,2048]{2,1,0:T(1,128)S(1)}, u32[]{:S(2)}) copy-start(f32[55,1,2048]{2,1,0:T(1,128)S(1)} %divide_add_fusion) | copy-start | bytes 1351684
  124.6 19.4 %collective-permute-start.2 = (f32[55,1,2048]{2,1,0:T(1,128)S(1)}, f32[55,1,2048]{2,1,0:T(1,128)S(1)}, u32[]{:S(2)}, u32[]{:S(2)}) collective-permute-start(f32[55,1,2048]{2,1,0:T(1,128)S(1)} %divide_add_fusion), channel_id=1, source_target_pairs={{4,0},{8,4},{12,8},{16,12},{20,16},{24,20},{28,24},{32,28},{36,32}... | collective-permute-start | bytes 1351688 | tf_op jit(solution)/shard_map/ppermute | solution.py:25
  127.7 27.5 %collective-permute-start.3 = (f32[55,1,2048]{2,1,0:T(1,128)S(1)}, f32[55,1,2048]{2,1,0:T(1,128)S(1)}, u32[]{:S(2)}, u32[]{:S(2)}) collective-permute-start(f32[55,1,2048]{2,1,0:T(1,128)S(1)} %divide_add_fusion), channel_id=1, source_target_pairs={{0,4},{4,8},{8,12},{12,16},{16,20},{20,24},{24,28},{28,32},{32,36}... | collective-permute-start | bytes 1351688 | tf_op jit(solution)/shard_map/ppermute | solution.py:22
  160.9 3.9 %copy-start.7 = (s32[512,9]{0,1:T(8,128)S(1)}, s32[512,9]{0,1:T(8,128)}, u32[]{:S(2)}) copy-start(s32[512,9]{0,1:T(8,128)} %param.16) | copy-start | bytes 55300
  160.9 35.2 %all-to-all-start = ((f32[4,3,55,1,512]{4,3,2,1,0:T(1,128)}), f32[4,3,55,1,512]{4,3,2,1,0:T(1,128)S(1)}, u32[]{:S(2)}, u32[]{:S(2)}) async-start(f32[4,3,55,1,512]{4,3,2,1,0:T(1,128)} %pad_maximum_fusion.2), calls=%async_computation | async-start | bytes 2703360 | tf_op jit(solution)/shard_map/all_to_all | solution.py:158
  196.1 1.1 copy-start.1
  199.9 6.3 %copy-start.11 = (pred[512]{0:T(512)(128)(4,1)S(1)}, pred[512]{0:T(512)(128)(4,1)}, u32[]{:S(2)}) copy-start(pred[512]{0:T(512)(128)(4,1)} %get-tuple-element.10) | copy-start | bytes 1540
  199.9 6.3 %copy-start.12 = (pred[512]{0:T(512)(128)(4,1)S(1)}, pred[512]{0:T(512)(128)(4,1)}, u32[]{:S(2)}) copy-start(pred[512]{0:T(512)(128)(4,1)} %get-tuple-element.11) | copy-start | bytes 1540
  199.9 6.3 %copy-start.13 = (pred[512]{0:T(512)(128)(4,1)S(1)}, pred[512]{0:T(512)(128)(4,1)}, u32[]{:S(2)}) copy-start(pred[512]{0:T(512)(128)(4,1)} %get-tuple-element.12) | copy-start | bytes 1540
  199.9 6.3 %copy-start.14 = (pred[512]{0:T(512)(128)(4,1)S(1)}, pred[512]{0:T(512)(128)(4,1)}, u32[]{:S(2)}) copy-start(pred[512]{0:T(512)(128)(4,1)} %get-tuple-element.13) | copy-start | bytes 1540
  199.9 6.3 %copy-start.15 = (pred[220]{0:T(512)(128)(4,1)S(1)}, pred[220]{0:T(512)(128)(4,1)}, u32[]{:S(2)}) copy-start(pred[220]{0:T(512)(128)(4,1)} %get-tuple-element.108) | copy-start | bytes 664
  199.9 6.3 %copy-start.16 = (pred[220]{0:T(512)(128)(4,1)S(1)}, pred[220]{0:T(512)(128)(4,1)}, u32[]{:S(2)}) copy-start(pred[220]{0:T(512)(128)(4,1)} %get-tuple-element.109) | copy-start | bytes 664
  199.9 6.3 %copy-start.17 = (pred[220]{0:T(512)(128)(4,1)S(1)}, pred[220]{0:T(512)(128)(4,1)}, u32[]{:S(2)}) copy-start(pred[220]{0:T(512)(128)(4,1)} %get-tuple-element.110) | copy-start | bytes 664
  210.6 16.8 %all-to-all-start.1 = ((f32[220,1,512]{2,1,0:T(1,128)}), f32[220,1,512]{2,1,0:T(1,128)S(1)}, u32[]{:S(2)}, u32[]{:S(2)}) async-start(f32[220,1,512]{2,1,0:T(1,128)} %copy.42), calls=%async_computation.1 | async-start | bytes 901120 | tf_op jit(solution)/shard_map/all_to_all | solution.py:182
  229.3 6.1 %copy-start.2 = (f32[55,1,2040]{2,0,1:T(8,128)S(1)}, f32[55,1,2040]{2,0,1:T(8,128)}, u32[]{:S(2)}) copy-start(f32[55,1,2040]{2,0,1:T(8,128)} %get-tuple-element.25) | copy-start | bytes 1346404
Sparse Core Ops, SparseCore 0:
  67.5 50.1 all-gather.2
